TPU v7x, 128 devices: a whole 4x4x4 slice. The times are simulated.
128 devices in a mesh: row: 8 (over x_lo, y), col: 16 (over x_hi, z, core).
Axes of the slice: x: 4 (x_hi: 2, x_lo: 2; x = x_hi * 2 + x_lo), y: 4, z: 4, core: 2. Of those that a mesh axis runs over, the one named last changes fastest.
Arguments:
- features: bfloat16 [262144, 256], P(('col', 'row')), may hold values from -6 to 6
- weight: bfloat16 [256, 256], replicated, may hold values from -0.375 to 0.375
- adj_rows: int32 [8, 16, 128], P('row', 'col'), may hold values from 0 to 255, as said below
- adj_cols: int32 [8, 16, 128], P('row', 'col'), may hold values from 0 to 127
- adj_blocks: bfloat16 [8, 16, 128, 128, 128], P('row', 'col'), as said below
- counts: int32 [8, 16], P('row', 'col'), may hold values from 1 to 128, as said below
- grad_out: bfloat16 [262144, 256], P(('col', 'row')), may hold values from -6 to 6
Outputs:
- out_col: bfloat16 [262144, 256], P(('col', 'row'))
- weight_grad: float32 [256, 256], replicated
Inputs may be any that keep to these rules, and one draw needn't show every extreme that they name: `adj_rows`: in every grid cell, slot k's block-row lies in [(k % 16) * 16, (k % 16 + 1) * 16), and no two slots of a cell share a block-row. At least one grid cell has all 128 slots live; live slots are the first counts of a cell. `adj_blocks`: each block holds nonnegative edge weights.
All inputs are finite; a program needn't handle non-finite values.
Results may differ from a plain program's by a relative error of at most 0.015.
Values may be sent and summed in bfloat16 or wider, within the bound.
No kernel may reach another device: no remote copies, remote signals or barrier semaphores. Data moves between devices by JAX's collectives and lax.ppermute only.
A program may use at most 128 MiB of HBM per device.

v0:
```python
import jax
import jax.numpy as jnp
from jax import lax
from jax.sharding import PartitionSpec as P

VBLK = 16


def group_products(col_blocks, slab_cols, blocks, live_count, first_slot, group):
    cols_here = lax.dynamic_slice_in_dim(slab_cols, first_slot, group)
    blocks_here = lax.dynamic_slice_in_dim(blocks, first_slot, group, 0)
    live_mask = first_slot + jnp.arange(group) < live_count
    picked = col_blocks[cols_here]
    products = jnp.einsum("kil,klf->kif", blocks_here, picked, preferred_element_type=jnp.float32)
    return jnp.where(live_mask[:, None, None], products, 0.0).astype(jnp.bfloat16)


def dense_partial(col_blocks, slab_rows, slab_cols, blocks, live_count, row_blocks, group):
    block_size = blocks.shape[-1]
    feat_width = col_blocks.shape[-1]
    turns = (live_count + group - 1) // group

    def one_group(group_idx, running):
        first_slot = group_idx * group
        rows_here = lax.dynamic_slice_in_dim(slab_rows, first_slot, group)
        products = group_products(col_blocks, slab_cols, blocks, live_count, first_slot, group)
        return running.at[rows_here].add(products)

    start_value = jnp.zeros((row_blocks, block_size, feat_width), jnp.bfloat16)
    running = lax.fori_loop(0, turns, one_group, start_value)
    return running.reshape(row_blocks * block_size, feat_width)


def derivative(preact, grad_rows):
    sigmoid_pre = jax.nn.sigmoid(preact)
    return (
        grad_rows.astype(jnp.float32) * sigmoid_pre * (1.0 + preact * (1.0 - sigmoid_pre))
    ).astype(jnp.bfloat16)


def on_device(features, weight, adj_rows, adj_cols, adj_blocks, counts, grad_out):
    feat_width = features.shape[1]
    local_rows = features.shape[0]
    owners = lax.axis_size("col")
    devices_all = lax.axis_size("row") * owners
    piece_rows = local_rows // devices_all
    block_size = adj_blocks.shape[-1]
    slot_total = adj_blocks.shape[2]
    group = min(32, slot_total)
    row_blocks = VBLK * owners
    slab = lax.all_gather(features, "row", axis=0, tiled=True)
    col_blocks = slab.reshape(-1, block_size, feat_width)
    slab_rows = adj_rows[0, 0]
    slab_cols = adj_cols[0, 0]
    blocks = adj_blocks[0, 0]
    live_count = counts[0, 0]
    partial_value = dense_partial(
        col_blocks, slab_rows, slab_cols, blocks, live_count, row_blocks, group
    )
    agg = (
        lax.psum_scatter(partial_value, "col", scatter_dimension=0, tiled=True)
        .astype(jnp.float32)
        .astype(jnp.bfloat16)
    )
    preact = jnp.dot(agg, weight, preferred_element_type=jnp.float32)
    out_row = jax.nn.silu(preact).astype(jnp.bfloat16)
    contract = (((0,), (0,)), ((), ()))
    moved = lax.all_to_all(
        out_row.reshape(devices_all, piece_rows, feat_width),
        ("row", "col"),
        split_axis=0,
        concat_axis=0,
        tiled=True,
    )
    out_col = moved.reshape(local_rows, feat_width)
    grad_row = lax.all_to_all(
        grad_out.reshape(devices_all, piece_rows, feat_width),
        ("row", "col"),
        split_axis=0,
        concat_axis=0,
        tiled=True,
    )
    grad_pre = derivative(preact, grad_row.reshape(local_rows, feat_width))
    weight_part = lax.dot_general(agg, grad_pre, contract, preferred_element_type=jnp.float32)
    weight_grad = lax.psum(weight_part, ("row", "col")) * (local_rows * devices_all) ** (-0.5)
    return (out_col, weight_grad)


def solution(mesh):
    placed = (
        P(("col", "row"), None),
        P(),
        P("row", "col", None),
        P("row", "col", None),
        P("row", "col", None, None, None),
        P("row", "col"),
        P(("col", "row"), None),
    )
    return jax.shard_map(
        on_device,
        mesh=mesh,
        in_specs=placed,
        out_specs=(P(("col", "row"), None), P()),
        check_vma=False,
    )
```

profile of v0, /device:TPU:1, one launch (start us, length us, event | category | flops | bytes accessed | tf_op | source)
XLA Modules:
  0.0 496.6 jit_solution(323156815200104506)
XLA Ops:
  7.2 0.0 copy-start
  7.2 0.0 all-gather.2.cloned.1.call-start
  7.2 0.7 all-gather.2.cloned.1.call-update
  7.9 0.0 reduce-scatter.2.cloned.1.call-start
  8.6 96.2 %all-gather.2.cloned.1.call-done = bf16[16384,256]{1,0:T(8,128)(2,1)} async-done(((bf16[2048,256]{1,0:T(8,128)(2,1)}), bf16[16384,256]{1,0:T(8,128)(2,1)}) %all-gather.2.cloned.1.call-update) | async-done | bytes 8388624 | tf_op jit(solution)/shard_map/all_gather | solution.py:51
  104.8 0.0 copy-start.3
  104.8 0.0 copy-start.4
  104.8 6.0 %broadcast_in_dim.22 = bf16[256,128,256]{2,1,0:T(8,128)(2,1)} broadcast(bf16[]{:T(256)} %constant.35.clone.1), dimensions={} | broadcast | bytes 16777218 | tf_op jit(solution)/shard_map/broadcast_in_dim | solution.py:29
  110.8 0.0 copy-done.3
  110.8 0.0 copy-done.4
  110.8 72.3 %while.10 = (s32[]{:T(128)}, bf16[256,128,256]{2,1,0:T(8,128)(2,1)}, s32[]{:T(128)}, s32[128]{0:T(128)S(1)}, s32[]{:T(128)}, /*index=5*/bf16[128,128,128]{2,1,0:...) while((s32[]{:T(128)}, ...), condition=%wide.region_2.3_spmd, body=%wide.region_0.2_spmd.sunk | while | flops 271582464 | bytes 15733875 | solution.py:30
  110.8 0.1 compare_select_fusion.3
  110.9 5.4 %gather_fusion = bf16[32,128,256]{2,1,0:T(8,128)(2,1)} fusion(bf16[128,128,256]{2,1,0:T(8,128)(2,1)} %get-tuple-element.151, s32[1024]{0:T(1024)S(1)} %pad_clamp_fusion.2), kind=kCustom, calls=%fused_computation.clone.1 | custom fusion | bytes 4194432 | tf_op jit(solution)/shard_map/while/body/gather | solution.py:13
  116.3 0.7 add_compare_fusion.2
  117.0 2.6 select_convert_fusion.2
  119.6 9.3 %scatter_fusion = bf16[256,128,256]{2,1,0:T(8,128)(2,1)} fusion(bf16[256,128,256]{2,1,0:T(8,128)(2,1)} %get-tuple-element.133, s32[32]{0:T(128)S(1)} %get-tuple-element.118, bf16[32,128,256]{2,1,0:T(8,128)(2,1)S(1)} %select_convert_fusion.2), kind=kCustom, calls=%fused_computation.1.clone.1 | custom fusion | flops 1048576 | bytes 6291584 | tf_op jit(solution)/shard_map/while/body/scatter-add | solution.py:27
  128.9 0.1 compare_select_fusion.3
  129.0 5.4 %gather_fusion = bf16[32,128,256]{2,1,0:T(8,128)(2,1)} fusion(bf16[128,128,256]{2,1,0:T(8,128)(2,1)} %get-tuple-element.151, s32[1024]{0:T(1024)S(1)} %pad_clamp_fusion.2), kind=kCustom, calls=%fused_computation.clone.1 | custom fusion | bytes 4194432 | tf_op jit(solution)/shard_map/while/body/gather | solution.py:13
  134.4 0.7 add_compare_fusion.2
  135.1 2.6 select_convert_fusion.2
  137.7 9.3 %scatter_fusion = bf16[256,128,256]{2,1,0:T(8,128)(2,1)} fusion(bf16[256,128,256]{2,1,0:T(8,128)(2,1)} %get-tuple-element.133, s32[32]{0:T(128)S(1)} %get-tuple-element.118, bf16[32,128,256]{2,1,0:T(8,128)(2,1)S(1)} %select_convert_fusion.2), kind=kCustom, calls=%fused_computation.1.clone.1 | custom fusion | flops 1048576 | bytes 6291584 | tf_op jit(solution)/shard_map/while/body/scatter-add | solution.py:27
  147.0 0.1 compare_select_fusion.3
  147.1 5.4 %gather_fusion = bf16[32,128,256]{2,1,0:T(8,128)(2,1)} fusion(bf16[128,128,256]{2,1,0:T(8,128)(2,1)} %get-tuple-element.151, s32[1024]{0:T(1024)S(1)} %pad_clamp_fusion.2), kind=kCustom, calls=%fused_computation.clone.1 | custom fusion | bytes 4194432 | tf_op jit(solution)/shard_map/while/body/gather | solution.py:13
  152.5 0.7 add_compare_fusion.2
  153.1 2.6 select_convert_fusion.2
  155.8 9.3 %scatter_fusion = bf16[256,128,256]{2,1,0:T(8,128)(2,1)} fusion(bf16[256,128,256]{2,1,0:T(8,128)(2,1)} %get-tuple-element.133, s32[32]{0:T(128)S(1)} %get-tuple-element.118, bf16[32,128,256]{2,1,0:T(8,128)(2,1)S(1)} %select_convert_fusion.2), kind=kCustom, calls=%fused_computation.1.clone.1 | custom fusion | flops 1048576 | bytes 6291584 | tf_op jit(solution)/shard_map/while/body/scatter-add | solution.py:27
  165.1 0.1 compare_select_fusion.3
  165.2 5.4 %gather_fusion = bf16[32,128,256]{2,1,0:T(8,128)(2,1)} fusion(bf16[128,128,256]{2,1,0:T(8,128)(2,1)} %get-tuple-element.151, s32[1024]{0:T(1024)S(1)} %pad_clamp_fusion.2), kind=kCustom, calls=%fused_computation.clone.1 | custom fusion | bytes 4194432 | tf_op jit(solution)/shard_map/while/body/gather | solution.py:13
  170.6 0.7 add_compare_fusion.2
  171.2 2.6 select_convert_fusion.2
  173.9 9.2 %scatter_fusion = bf16[256,128,256]{2,1,0:T(8,128)(2,1)} fusion(bf16[256,128,256]{2,1,0:T(8,128)(2,1)} %get-tuple-element.133, s32[32]{0:T(128)S(1)} %get-tuple-element.118, bf16[32,128,256]{2,1,0:T(8,128)(2,1)S(1)} %select_convert_fusion.2), kind=kCustom, calls=%fused_computation.1.clone.1 | custom fusion | flops 1048576 | bytes 6291584 | tf_op jit(solution)/shard_map/while/body/scatter-add | solution.py:27
  183.1 0.0 copy-start.1
  183.1 0.0 reduce-scatter.2.cloned.1.call-update
  183.1 1.2 copy-done.1
  184.3 26.0 %all_to_all.10 = bf16[128,16,256]{2,1,0:T(8,128)(2,1)S(1)} all-to-all(bf16[128,16,256]{2,1,0:T(8,128)(2,1)S(1)} %bitcast.24), channel_id=1, replica_groups=mesh['row'=8,'col'=16] {'row','col'}, dimensions={0} | all-to-all | bytes 2097152 | tf_op jit(solution)/shard_map/all_to_all | solution.py:76
  210.3 117.8 %reduce-scatter.2.cloned.1.call-done = bf16[2048,256]{1,0:T(8,128)(2,1)} async-done(((bf16[32768,256]{1,0:T(8,128)(2,1)}), bf16[2048,256]{1,0:T(8,128)(2,1)}) %reduce-scatter.2.cloned.1.call-update) | async-done | bytes 1048592 | tf_op jit(solution)/shard_map/reduce_scatter | solution.py:61
  328.1 0.0 copy-done
  328.1 3.4 fusion.3
  331.5 0.0 copy-start.2
  331.5 6.7 %all-to-all-start = ((bf16[128,16,256]{2,1,0:T(8,128)(2,1)}), bf16[128,16,256]{2,1,0:T(8,128)(2,1)S(1)}, u32[]{:S(2)}, u32[]{:S(2)}) async-start(bf16[128,16,256]{2,1,0:T(8,128)(2,1)} %bitcast.6), calls=%async_computation.1 | async-start | bytes 2097152 | tf_op jit(solution)/shard_map/all_to_all | solution.py:68
  338.2 0.0 all-reduce.2.cloned.1.call-start
  338.2 0.0 copy-done.2
  338.2 1.2 fusion.4
  339.4 0.0 all-reduce.2.cloned.1.call-update
  339.4 148.0 %all-reduce.2.cloned.1.call-done = f32[256,256]{1,0:T(8,128)} async-done(((f32[256,256]{1,0:T(8,128)}), f32[256,256]{1,0:T(8,128)}) %all-reduce.2.cloned.1.call-update) | async-done | bytes 262160 | tf_op jit(solution)/shard_map/psum | solution.py:85
  487.4 1.7 broadcast_multiply_fusion
  489.1 0.0 all-to-all-done
  489.1 1.0 copy.19
  (4 shorter events, 0.0 us)
Async XLA Ops:
  7.2 321.0 %copy-start = (bf16[256,256]{1,0:T(8,128)(2,1)S(1)}, bf16[256,256]{1,0:T(8,128)(2,1)}, u32[]{:S(2)}) copy-start(bf16[256,256]{1,0:T(8,128)(2,1)} %param.10) | copy-start | bytes 393220
  7.2 97.6 %all-gather.2.cloned.1.call-start = ((), (), s32[]{:S(2)}) async-start(), calls=%async_computation.3 | async-start | bytes 9437184 | tf_op jit(solution)/shard_map/all_gather | solution.py:51
  7.9 320.2 %reduce-scatter.2.cloned.1.call-start = ((), (), s32[]{:S(2)}) async-start(), calls=%async_computation.4 | async-start | bytes 17825792 | tf_op jit(solution)/shard_map/reduce_scatter | solution.py:61
  104.8 6.0 %copy-start.3 = (s32[1,1,128]{2,1,0:T(1,128)S(1)}, s32[1,1,128]{2,1,0:T(1,128)}, u32[]{:S(2)}) copy-start(s32[1,1,128]{2,1,0:T(1,128)} %param.11) | copy-start | bytes 1540
  104.8 6.0 %copy-start.4 = (s32[1,1,128]{2,1,0:T(1,128)S(1)}, s32[1,1,128]{2,1,0:T(1,128)}, u32[]{:S(2)}) copy-start(s32[1,1,128]{2,1,0:T(1,128)} %param.12) | copy-start | bytes 1540
  183.1 1.2 copy-start.1
  331.5 6.7 %copy-start.2 = (bf16[2048,256]{1,0:T(8,128)(2,1)S(1)}, bf16[2048,256]{1,0:T(8,128)(2,1)}, u32[]{:S(2)}) copy-start(bf16[2048,256]{1,0:T(8,128)(2,1)} %reduce-scatter.2.cloned.1.call-done) | copy-start | bytes 3145732
  331.5 157.6 %all-to-all-start = ((bf16[128,16,256]{2,1,0:T(8,128)(2,1)}), bf16[128,16,256]{2,1,0:T(8,128)(2,1)S(1)}, u32[]{:S(2)}, u32[]{:S(2)}) async-start(bf16[128,16,256]{2,1,0:T(8,128)(2,1)} %bitcast.6), calls=%async_computation.1 | async-start | bytes 2097152 | tf_op jit(solution)/shard_map/all_to_all | solution.py:68
  338.2 149.3 %all-reduce.2.cloned.1.call-start = ((), (), s32[]{:S(2)}) async-start(), calls=%async_computation.5 | async-start | bytes 524288 | tf_op jit(solution)/shard_map/psum | solution.py:85
Sparse Core Ops, SparseCore 0:
  9.7 95.1 all-gather.1
  183.3 144.8 reduce-scatter.1
  344.3 143.0 all-reduce.1
where the time goes:
time: 498 us; the launch traced here: 497 us
  waiting for transfers between devices  363 us (73%)
  other arithmetic  41.8 us (8%)
  local copies, waits for them, and re-layouts  29.9 us (6%)
  blocking collectives  26 us (5%)
  matrix products  15 us (3%)
  between operations  14.4 us (3%)
  starting transfers between devices  6.78 us (1%)
    psum x1, waiting for transfers between devices, on_device(): lax.psum(weight_part, ('row', 'col')) * (local_rows * devices_all) ** (-0.5)  148 us
    reduce_scatter x1, waiting for transfers between devices, on_device(): lax.psum_scatter(partial_value, 'col', scatter_dimension=0, tiled=True)  118 us
    all_gather x1, waiting for transfers between devices, on_device(): slab = lax.all_gather(features, 'row', axis=0, tiled=True)  96.2 us
    scatter-add x4, other arithmetic, one_group(): return running.at[rows_here].add(products)  37.2 us
    all_to_all x1, blocking collectives, on_device(): lax.all_to_all(grad_out.reshape(devices_all, piece_rows, feat_width), ('r...  26 us
    gather x4, local copies, waits for them, and re-layouts, group_products(): picked = col_blocks[cols_here]  21.7 us
    dot_general x4, matrix products, group_products(): jnp.einsum('kil,klf->kif', blocks_here, picked, preferred_element_type=jn...  10.5 us
  transfers between devices with their start and end apart: 4, of which 3 were waited for; matrix products, arithmetic and copies ran while one was open for 1% of the time, Pallas kernels for 0%

commit v1 on v0

--- a/solution.py
+++ b/solution.py
@@ -82,7 +82,9 @@
     )
     grad_pre = derivative(preact, grad_row.reshape(local_rows, feat_width))
     weight_part = lax.dot_general(agg, grad_pre, contract, preferred_element_type=jnp.float32)
-    weight_grad = lax.psum(weight_part, ("row", "col")) * (local_rows * devices_all) ** (-0.5)
+    weight_grad = lax.psum(lax.psum(weight_part, "row"), "col") * (local_rows * devices_all) ** (
+        -0.5
+    )
     return (out_col, weight_grad)
 
 

time: 498 us -> 568 us (1.14)
  waiting for transfers between devices: 363 us -> 433 us
    psum x1 -> x2, waiting for transfers between devices: 148 us -> 218 us  [the longest x1 145 us: on_device(): lax.psum(lax.psum(weight_part, 'row'), 'col')]
  transfers between devices with their start and end apart: 4 -> 5, of which waited for: 3 -> 4; matrix products, arithmetic and copies ran while one was open for 1% -> 1% of each run, Pallas kernels for 0% -> 0%
where the time goes in v1:
time: 568 us; the launch traced here: 567 us
  waiting for transfers between devices  433 us (76%)
  other arithmetic  41.8 us (7%)
  local copies, waits for them, and re-layouts  29.9 us (5%)
  blocking collectives  26 us (5%)
  matrix products  15 us (3%)
  between operations  14.5 us (3%)
  starting transfers between devices  6.83 us (1%)
    psum x1, waiting for transfers between devices, on_device(): lax.psum(lax.psum(weight_part, 'row'), 'col')  145 us
    reduce_scatter x1, waiting for transfers between devices, on_device(): lax.psum_scatter(partial_value, 'col', scatter_dimension=0, tiled=True)  118 us
    all_gather x1, waiting for transfers between devices, on_device(): slab = lax.all_gather(features, 'row', axis=0, tiled=True)  96.2 us
    psum x1, waiting for transfers between devices, on_device(): lax.psum(weight_part, 'row')  73 us
    scatter-add x4, other arithmetic, one_group(): return running.at[rows_here].add(products)  37.2 us
    all_to_all x1, blocking collectives, on_device(): lax.all_to_all(grad_out.reshape(devices_all, piece_rows, feat_width), ('r...  26 us
    gather x4, local copies, waits for them, and re-layouts, group_products(): picked = col_blocks[cols_here]  21.7 us
  transfers between devices with their start and end apart: 5, of which 4 were waited for; matrix products, arithmetic and copies ran while one was open for 1% of the time, Pallas kernels for 0%

profile of v1, /device:TPU:1, one launch (start us, length us, event | category | flops | bytes accessed | tf_op | source)
XLA Modules:
  0.0 566.5 jit_solution(4875075800408725251)
XLA Ops:
  7.2 0.0 copy-start
  7.2 0.0 all-gather.2.cloned.1.call-start
  7.2 0.7 all-gather.2.cloned.1.call-update
  7.9 0.0 reduce-scatter.2.cloned.1.call-start
  8.6 96.2 %all-gather.2.cloned.1.call-done = bf16[16384,256]{1,0:T(8,128)(2,1)} async-done(((bf16[2048,256]{1,0:T(8,128)(2,1)}), bf16[16384,256]{1,0:T(8,128)(2,1)}) %all-gather.2.cloned.1.call-update) | async-done | bytes 8388624 | tf_op jit(solution)/shard_map/all_gather | solution.py:51
  104.8 0.0 copy-start.3
  104.8 6.0 %broadcast_in_dim.22 = bf16[256,128,256]{2,1,0:T(8,128)(2,1)} broadcast(bf16[]{:T(256)} %constant.35.clone.1), dimensions={} | broadcast | bytes 16777218 | tf_op jit(solution)/shard_map/broadcast_in_dim | solution.py:29
  110.8 0.0 copy-done.3
  110.8 0.0 copy-done.4
  110.8 72.3 %while.10 = (s32[]{:T(128)}, bf16[256,128,256]{2,1,0:T(8,128)(2,1)}, s32[]{:T(128)}, s32[128]{0:T(128)S(1)}, s32[]{:T(128)}, /*index=5*/bf16[128,128,128]{2,1,0:...) while((s32[]{:T(128)}, ...), condition=%wide.region_2.3_spmd, body=%wide.region_0.2_spmd.sunk | while | flops 271582464 | bytes 15733875 | solution.py:30
  110.8 0.1 compare_select_fusion.3
  110.9 5.4 gather_fusion
  116.3 0.7 add_compare_fusion.2
  117.0 2.6 select_convert_fusion.2
  119.6 9.3 %scatter_fusion = bf16[256,128,256]{2,1,0:T(8,128)(2,1)} fusion(bf16[256,128,256]{2,1,0:T(8,128)(2,1)} %get-tuple-element.133, s32[32]{0:T(128)S(1)} %get-tuple-element.118, bf16[32,128,256]{2,1,0:T(8,128)(2,1)S(1)} %select_convert_fusion.2), kind=kCustom, calls=%fused_computation.1.clone.1 | custom fusion | flops 1048576 | bytes 6291584 | tf_op jit(solution)/shard_map/while/body/scatter-add | solution.py:27
  128.9 0.1 compare_select_fusion.3
  129.0 5.4 gather_fusion
  134.4 0.7 add_compare_fusion.2
  135.1 2.6 select_convert_fusion.2
  137.7 9.3 %scatter_fusion = bf16[256,128,256]{2,1,0:T(8,128)(2,1)} fusion(bf16[256,128,256]{2,1,0:T(8,128)(2,1)} %get-tuple-element.133, s32[32]{0:T(128)S(1)} %get-tuple-element.118, bf16[32,128,256]{2,1,0:T(8,128)(2,1)S(1)} %select_convert_fusion.2), kind=kCustom, calls=%fused_computation.1.clone.1 | custom fusion | flops 1048576 | bytes 6291584 | tf_op jit(solution)/shard_map/while/body/scatter-add | solution.py:27
  147.0 0.1 compare_select_fusion.3
  147.1 5.4 gather_fusion
  152.5 0.7 add_compare_fusion.2
  153.1 2.6 select_convert_fusion.2
  155.8 9.3 %scatter_fusion = bf16[256,128,256]{2,1,0:T(8,128)(2,1)} fusion(bf16[256,128,256]{2,1,0:T(8,128)(2,1)} %get-tuple-element.133, s32[32]{0:T(128)S(1)} %get-tuple-element.118, bf16[32,128,256]{2,1,0:T(8,128)(2,1)S(1)} %select_convert_fusion.2), kind=kCustom, calls=%fused_computation.1.clone.1 | custom fusion | flops 1048576 | bytes 6291584 | tf_op jit(solution)/shard_map/while/body/scatter-add | solution.py:27
  165.1 0.1 compare_select_fusion.3
  165.2 5.4 gather_fusion
  170.6 0.7 add_compare_fusion.2
  171.2 2.6 select_convert_fusion.2
  173.9 9.2 %scatter_fusion = bf16[256,128,256]{2,1,0:T(8,128)(2,1)} fusion(bf16[256,128,256]{2,1,0:T(8,128)(2,1)} %get-tuple-element.133, s32[32]{0:T(128)S(1)} %get-tuple-element.118, bf16[32,128,256]{2,1,0:T(8,128)(2,1)S(1)} %select_convert_fusion.2), kind=kCustom, calls=%fused_computation.1.clone.1 | custom fusion | flops 1048576 | bytes 6291584 | tf_op jit(solution)/shard_map/while/body/scatter-add | solution.py:27
  183.1 0.0 reduce-scatter.2.cloned.1.call-update
  183.1 1.2 copy-done.1
  184.3 26.0 %all_to_all.10 = bf16[128,16,256]{2,1,0:T(8,128)(2,1)S(1)} all-to-all(bf16[128,16,256]{2,1,0:T(8,128)(2,1)S(1)} %bitcast.24), channel_id=1, replica_groups=mesh['row'=8,'col'=16] {'row','col'}, dimensions={0} | all-to-all | bytes 2097152 | tf_op jit(solution)/shard_map/all_to_all | solution.py:76
  210.3 117.8 %reduce-scatter.2.cloned.1.call-done = bf16[2048,256]{1,0:T(8,128)(2,1)} async-done(((bf16[32768,256]{1,0:T(8,128)(2,1)}), bf16[2048,256]{1,0:T(8,128)(2,1)}) %reduce-scatter.2.cloned.1.call-update) | async-done | bytes 1048592 | tf_op jit(solution)/shard_map/reduce_scatter | solution.py:61
  328.1 0.0 copy-done
  328.1 3.4 fusion.3
  331.5 6.7 %all-to-all-start = ((bf16[128,16,256]{2,1,0:T(8,128)(2,1)}), bf16[128,16,256]{2,1,0:T(8,128)(2,1)S(1)}, u32[]{:S(2)}, u32[]{:S(2)}) async-start(bf16[128,16,256]{2,1,0:T(8,128)(2,1)} %bitcast.6), calls=%async_computation.1 | async-start | bytes 2097152 | tf_op jit(solution)/shard_map/all_to_all | solution.py:68
  338.2 0.0 all-reduce.3.cloned.1.call-start
  338.2 0.0 copy-done.2
  338.2 1.2 fusion.4
  339.4 0.0 all-reduce.3.cloned.1.call-update
  339.4 0.0 all-reduce.5.cloned.1.call-start
  339.5 73.0 %all-reduce.3.cloned.1.call-done = f32[256,256]{1,0:T(8,128)} async-done(((f32[256,256]{1,0:T(8,128)}), f32[256,256]{1,0:T(8,128)}) %all-reduce.3.cloned.1.call-update) | async-done | bytes 262160 | tf_op jit(solution)/shard_map/psum | solution.py:85
  412.5 0.0 all-reduce.5.cloned.1.call-update
  412.6 144.8 %all-reduce.5.cloned.1.call-done = f32[256,256]{1,0:T(8,128)} async-done(((f32[256,256]{1,0:T(8,128)}), f32[256,256]{1,0:T(8,128)}) %all-reduce.5.cloned.1.call-update) | async-done | bytes 262160 | tf_op jit(solution)/shard_map/psum | solution.py:85
  557.3 1.7 broadcast_multiply_fusion
  559.0 0.0 all-to-all-done
  559.0 1.0 copy.20
  (7 shorter events, 0.0 us)
Async XLA Ops:
  7.2 321.0 %copy-start = (bf16[256,256]{1,0:T(8,128)(2,1)S(1)}, bf16[256,256]{1,0:T(8,128)(2,1)}, u32[]{:S(2)}) copy-start(bf16[256,256]{1,0:T(8,128)(2,1)} %param.10) | copy-start | bytes 393220
  7.2 97.6 %all-gather.2.cloned.1.call-start = ((), (), s32[]{:S(2)}) async-start(), calls=%async_computation.3 | async-start | bytes 9437184 | tf_op jit(solution)/shard_map/all_gather | solution.py:51
  7.9 320.2 %reduce-scatter.2.cloned.1.call-start = ((), (), s32[]{:S(2)}) async-start(), calls=%async_computation.4 | async-start | bytes 17825792 | tf_op jit(solution)/shard_map/reduce_scatter | solution.py:61
  104.8 6.0 %copy-start.3 = (s32[1,1,128]{2,1,0:T(1,128)S(1)}, s32[1,1,128]{2,1,0:T(1,128)}, u32[]{:S(2)}) copy-start(s32[1,1,128]{2,1,0:T(1,128)} %param.11) | copy-start | bytes 1540
  104.8 6.0 %copy-start.4 = (s32[1,1,128]{2,1,0:T(1,128)S(1)}, s32[1,1,128]{2,1,0:T(1,128)}, u32[]{:S(2)}) copy-start(s32[1,1,128]{2,1,0:T(1,128)} %param.12) | copy-start | bytes 1540
  183.1 1.2 copy-start.1
  331.5 6.7 %copy-start.2 = (bf16[2048,256]{1,0:T(8,128)(2,1)S(1)}, bf16[2048,256]{1,0:T(8,128)(2,1)}, u32[]{:S(2)}) copy-start(bf16[2048,256]{1,0:T(8,128)(2,1)} %reduce-scatter.2.cloned.1.call-done) | copy-start | bytes 3145732
  331.5 227.5 %all-to-all-start = ((bf16[128,16,256]{2,1,0:T(8,128)(2,1)}), bf16[128,16,256]{2,1,0:T(8,128)(2,1)S(1)}, u32[]{:S(2)}, u32[]{:S(2)}) async-start(bf16[128,16,256]{2,1,0:T(8,128)(2,1)} %bitcast.6), calls=%async_computation.1 | async-start | bytes 2097152 | tf_op jit(solution)/shard_map/all_to_all | solution.py:68
  338.2 74.4 %all-reduce.3.cloned.1.call-start = ((), (), s32[]{:S(2)}) async-start(), calls=%async_computation.5 | async-start | bytes 524288 | tf_op jit(solution)/shard_map/psum | solution.py:85
  339.4 217.9 %all-reduce.5.cloned.1.call-start = ((), (), s32[]{:S(2)}) async-start(), calls=%async_computation.6 | async-start | bytes 524288 | tf_op jit(solution)/shard_map/psum | solution.py:85
Sparse Core Ops, SparseCore 0:
  9.7 95.1 all-gather.1
  183.3 144.8 reduce-scatter.1
  342.1 70.4 all-reduce.2
  415.0 142.2 all-reduce.4
